TPU v7x, 512 devices: a whole 4x8x8 slice. The times are simulated.
512 devices in a mesh: req: 64 (over y, x, core), tp: 8 (over z).
Axes of the slice: x: 4, y: 8, z: 8, core: 2. Of those that a mesh axis runs over, the one named last changes fastest.
Arguments:
- tokens: bfloat16 [13312, 2048], P('req', 'tp'), may hold values from -6 to 6
- ln_gain: bfloat16 [2048], P('tp'), may hold values from 0.099609375 to 1.8984375
- ln_bias: bfloat16 [2048], P('tp'), may hold values from -3 to 3
- w_qkv: bfloat16 [2048, 3, 1024], P(None, None, 'tp'), may hold values from -3 to 3
- qkv_bias: bfloat16 [3, 1024], P(None, 'tp'), may hold values from -3 to 3
- w_dense: bfloat16 [1024, 2048], P('tp'), may hold values from -0.1875 to 0.1875
- dense_bias: bfloat16 [2048], P('tp'), may hold values from -3 to 3
- prefix_kv: bfloat16 [1024, 32, 2, 1024], P('req', None, None, 'tp'), may hold values from -6 to 6
- lengths: int32 [64, 16], replicated, may hold values from 1 to 16, 208 in all within a row
- owner_slot: int32 [1024], replicated, may hold values from 0 to 1023, as said below
Outputs:
- attended: bfloat16 [13312, 2048], P('req', 'tp')
- new_cache: bfloat16 [1024, 16, 2, 1024], P('req', None, None, 'tp')
Inputs may be any that keep to these rules, and one draw needn't show every extreme that they name: owner_slot names every slot once; owner_slot[g] % 16 == g % 16; two requests of one req index name slots on the same req index only if their j differ by a multiple of 64, so one req index sends exactly 1 request to each req index that it sends to. `lengths`: each row sums to 208 and reaches 16.
All inputs are finite; a program needn't handle non-finite values.
Results may differ from a plain program's by a relative error of at most 0.014.
Values may be sent and summed in bfloat16 or wider, within the bound.
No kernel may reach another device: no remote copies, remote signals or barrier semaphores. Data moves between devices by JAX's collectives and lax.ppermute only.
A program may use at most 64 MiB of HBM per device.

v0:
```python
import math
import jax
import jax.numpy as jnp
from jax import lax
from jax.sharding import PartitionSpec as P

D = 2048
HD = 128
HEADS = 8
LMAX = 16
PRE = 32


def moments_norm(values, total_one, total_two, gain_vec, shift_vec, width):
    mean_val = total_one[:, None] / width
    second = total_two[:, None] / width
    scale_inv = lax.rsqrt(second - mean_val * mean_val + 1e-05)
    return (
        (values - mean_val) * scale_inv * gain_vec.astype(jnp.float32)
        + shift_vec.astype(jnp.float32)
    ).astype(jnp.bfloat16)


def bucket_table(targets, count):
    return (targets[None, :] == jnp.arange(count, dtype=jnp.int32)[:, None]).astype(jnp.int32)


def attend(queries, all_keys, all_values, slopes, prefix_len):
    span = all_keys.shape[1]
    steps_new = queries.shape[1]
    scores = jnp.einsum(
        "rqhd,rkhd->rhqk", queries, all_keys, preferred_element_type=jnp.float32
    ) / math.sqrt(HD)
    distance = (prefix_len + jnp.arange(steps_new, dtype=jnp.int32))[:, None] - jnp.arange(
        span, dtype=jnp.int32
    )[None, :]
    scores = scores - slopes[None, :, None, None] * distance.astype(jnp.float32)[None, None]
    scores = jnp.where((distance >= 0)[None, None], scores, -jnp.inf)
    row_max = jnp.max(scores, axis=-1, keepdims=True)
    raised = jnp.exp(scores - row_max)
    weights = (raised / jnp.sum(raised, axis=-1, keepdims=True)).astype(jnp.bfloat16)
    return jnp.einsum(
        "rhqk,rkhd->rqhd", weights, all_values, preferred_element_type=jnp.float32
    ).astype(jnp.bfloat16)


def per_device(
    tokens, ln_gain, ln_bias, w_qkv, qkv_bias, w_dense, dense_bias, prefix_kv, lengths, owner_slot
):
    shards = lax.axis_size("req")
    req_rank = lax.axis_index("req")
    tp_rank = lax.axis_index("tp")
    tok_dev, part_cols = tokens.shape
    reqs_dev = lengths.shape[1]
    per_peer = max(1, reqs_dev // shards)
    buckets = shards * per_peer
    head_cols = w_dense.shape[0]
    heads_here = head_cols // HD
    slot_ids = jnp.arange(reqs_dev, dtype=jnp.int32)
    positions = jnp.arange(LMAX, dtype=jnp.int32)
    owners = (owner_slot // reqs_dev).reshape(shards, reqs_dev)
    own_sizes = lax.dynamic_index_in_dim(lengths, req_rank, 0, keepdims=False)
    own_starts = jnp.cumsum(own_sizes) - own_sizes
    own_dest = lax.dynamic_index_in_dim(owners, req_rank, 0, keepdims=False)
    send_bucket = own_dest * per_peer + slot_ids // shards
    send_table = bucket_table(send_bucket, buckets)
    bucket_start = jnp.sum(send_table * own_starts[None, :], axis=1)
    bucket_size = jnp.sum(send_table * own_sizes[None, :], axis=1)
    row_index = jnp.minimum(bucket_start[:, None] + positions[None, :], tok_dev - 1).reshape(-1)
    row_valid = (positions[None, :] < bucket_size[:, None]).reshape(-1, 1)
    outgoing = jnp.where(
        row_valid, jnp.take(tokens, row_index, axis=0), jnp.zeros((), tokens.dtype)
    )
    incoming = lax.all_to_all(
        outgoing.reshape(shards, per_peer * LMAX, part_cols),
        "req",
        split_axis=0,
        concat_axis=0,
        tiled=True,
    )
    owned_here = (owners == req_rank).astype(jnp.int32)
    source_of = jnp.sum(owned_here * jnp.arange(shards, dtype=jnp.int32)[:, None], axis=0)
    slot_sizes = jnp.sum(owned_here * lengths, axis=0)
    arrival = source_of * per_peer + slot_ids // shards
    slot_rows = (arrival[:, None] * LMAX + positions[None, :]).reshape(-1)
    local_rows = jnp.take(incoming.reshape(-1, part_cols), slot_rows, axis=0)
    slot_valid = positions[None, :] < slot_sizes[:, None]
    qkv_matrix = w_qkv.reshape(w_qkv.shape[0], -1)
    count_rows = reqs_dev * LMAX
    whole_rows, whole_gain, whole_shift = (
        lax.all_gather(local_rows, "tp", axis=1, tiled=True),
        lax.all_gather(ln_gain, "tp", axis=0, tiled=True),
        lax.all_gather(ln_bias, "tp", axis=0, tiled=True),
    )
    values = whole_rows.astype(jnp.float32)
    normed = moments_norm(
        values,
        jnp.sum(values, axis=1),
        jnp.sum(values * values, axis=1),
        whole_gain,
        whole_shift,
        D,
    )
    projected = jnp.dot(normed, qkv_matrix, preferred_element_type=jnp.float32)
    projected = (projected + qkv_bias.reshape(-1).astype(jnp.float32)).reshape(
        reqs_dev, LMAX, 3, heads_here, HD
    )
    live_mask = slot_valid[:, :, None, None]
    queries = projected[:, :, 0].astype(jnp.bfloat16)
    new_keys = jnp.where(live_mask, projected[:, :, 1], 0.0).astype(jnp.bfloat16)
    new_vals = jnp.where(live_mask, projected[:, :, 2], 0.0).astype(jnp.bfloat16)
    stored = prefix_kv.reshape(reqs_dev, PRE, 2, heads_here, HD)
    all_keys = jnp.concatenate([stored[:, :, 0], new_keys], axis=1)
    all_values = jnp.concatenate([stored[:, :, 1], new_vals], axis=1)
    head_ids = tp_rank * heads_here + jnp.arange(heads_here, dtype=jnp.int32) + 1
    slopes = jnp.exp2(-4.0 * head_ids.astype(jnp.float32) / HEADS)
    context = attend(queries, all_keys, all_values, slopes, PRE)
    new_cache = jnp.stack(
        [new_keys.reshape(reqs_dev, LMAX, head_cols), new_vals.reshape(reqs_dev, LMAX, head_cols)],
        axis=2,
    )
    flat_context = context.reshape(count_rows, head_cols)
    back_table = bucket_table(arrival, buckets)
    back_slot = jnp.sum(back_table * slot_ids[None, :], axis=1)
    back_rows = (back_slot[:, None] * LMAX + positions[None, :]).reshape(-1)
    tok_ids = jnp.arange(tok_dev, dtype=jnp.int32)
    token_req = jnp.sum((tok_ids[:, None] >= own_starts[None, :]).astype(jnp.int32), axis=1) - 1
    req_table = (token_req[:, None] == slot_ids[None, :]).astype(jnp.int32)
    home_index = jnp.sum(req_table * (send_bucket * LMAX - own_starts)[None, :], axis=1) + tok_ids
    partial_value = jnp.dot(flat_context, w_dense, preferred_element_type=jnp.float32)
    summed = lax.psum_scatter(
        partial_value.astype(jnp.bfloat16), "tp", scatter_dimension=1, tiled=True
    ).astype(jnp.float32)
    finished = (summed + dense_bias.astype(jnp.float32)).astype(jnp.bfloat16)
    outbound = jnp.take(finished, back_rows, axis=0).reshape(
        shards, per_peer * LMAX, finished.shape[1]
    )
    returned = lax.all_to_all(outbound, "req", split_axis=0, concat_axis=0, tiled=True)
    output = jnp.take(returned.reshape(-1, returned.shape[2]), home_index, axis=0)
    return (output, new_cache)


def solution(mesh):
    return jax.shard_map(
        per_device,
        mesh=mesh,
        in_specs=(
            P("req", "tp"),
            P("tp"),
            P("tp"),
            P(None, None, "tp"),
            P(None, "tp"),
            P("tp", None),
            P("tp"),
            P("req", None, None, "tp"),
            P(),
            P(),
        ),
        out_specs=(P("req", "tp"), P("req", None, None, "tp")),
        check_vma=False,
    )
```

profile of v0, /device:TPU:1, one launch (start us, length us, event | category | flops | bytes accessed | tf_op | source)
XLA Modules:
  0.0 178.7 jit_solution(6938996766615749987)
XLA Ops:
  7.2 0.9 copy.35
  8.1 0.2 reduce-window_clone.1
  8.3 0.7 add_select_fusion
  9.0 0.1 reshape.450
  9.1 0.1 select_reduce_fusion.1
  9.2 0.1 add_minimum_fusion
  9.3 0.1 iota_compare_fusion.1
  9.4 0.1 min.22
  9.5 3.9 %gather_fusion = bf16[1024,256]{1,0:T(8,128)(2,1)S(1)} fusion(bf16[208,256]{1,0:T(8,128)(2,1)S(1)} %copy-done.1, s32[1024]{0:T(1024)S(1)} %broadcast_clamp_fusion.1), kind=kCustom, calls=%fused_computation | custom fusion | bytes 1052672 | tf_op jit(solution)/shard_map/jit(_take)/gather | solution.py:72
  13.4 1.1 select_select_fusion
  14.6 11.7 %all-to-all-start = ((bf16[64,16,256]{2,1,0:T(8,128)(2,1)}), bf16[64,16,256]{2,1,0:T(8,128)(2,1)S(1)}, u32[]{:S(2)}, u32[]{:S(2)}) async-start(bf16[64,16,256]{2,1,0:T(8,128)(2,1)} %select_select_fusion), calls=%async_computation | async-start | bytes 1048576 | tf_op jit(solution)/shard_map/all_to_all | solution.py:74
  26.4 0.1 iota_add_fusion.1
  26.5 0.1 add.290
  26.6 0.1 add.281
  26.7 17.3 %all-to-all-done = bf16[64,16,256]{2,1,0:T(8,128)(2,1)S(1)} async-done(((bf16[64,16,256]{2,1,0:T(8,128)(2,1)}), bf16[64,16,256]{2,1,0:T(8,128)(2,1)S(1)}, u32[]{:S(2)}, u32[]{:S(2)}) %all-to-all-start) | async-done | bytes 524320 | tf_op jit(solution)/shard_map/all_to_all | solution.py:74
  44.0 1.2 gather_fusion.1
  45.2 0.8 broadcast_select_fusion.1
  46.0 1.6 copy.38
  47.6 18.9 %all-gather = bf16[8,1,256]{2,1,0:T(2,128)(2,1)S(1)} all-gather(bf16[1,1,256]{2,1,0:T(2,128)(2,1)S(1)} %reshape.492), channel_id=1, replica_groups=mesh['req'=64,'tp'=8] {'tp'}, dimensions={0}, use_global_device_ids=true | all-gather | bytes 4608 | tf_op jit(solution)/shard_map/all_gather | solution.py:92
  66.5 10.7 %all-gather.1 = bf16[8,1,256]{2,1,0:T(2,128)(2,1)S(1)} all-gather(bf16[1,1,256]{2,1,0:T(2,128)(2,1)S(1)} %reshape.494), channel_id=1, replica_groups=mesh['req'=64,'tp'=8] {'tp'}, dimensions={0}, use_global_device_ids=true | all-gather | bytes 4608 | tf_op jit(solution)/shard_map/all_gather | solution.py:93
  77.3 0.1 iota_compare_fusion.5
  77.4 0.1 fusion.26
  77.5 0.1 convert_multiply_fusion.1
  77.6 6.5 %all-gather.4.cloned.1.call-done = bf16[256,2048]{1,0:T(8,128)(2,1)} async-done(((bf16[256,256]{1,0:T(8,128)(2,1)}), bf16[256,2048]{1,0:T(8,128)(2,1)}) %all-gather.4.cloned.1.call-update) | async-done | bytes 1048592 | tf_op jit(solution)/shard_map/all_gather | solution.py:91
  84.1 1.7 convert_reduce_fusion
  85.8 2.0 %convolution_add_fusion = bf16[256,384]{1,0:T(8,128)(2,1)S(1)} fusion(bf16[2048,384]{0,1:T(8,128)(2,1)S(1)} %bitcast.64, bf16[256,2048]{1,0:T(8,128)(2,1)} %all-gather.4.cloned.1.call-done, f32[2048]{0:T(1024)S(1)} %bitcast.70, f32[2048]{0:T(1024)S(1)} %bitcast.69, f32[256]{0:T(256)S(1)} %get-tuple-element.28, f32[256]{0:T(256)S(1)} %get-tuple-element.27, ...), kind=kOutput, calls=%fused_computation.14 | convolution fusion | flops 405995520 | bytes 2838016 | tf_op jit(solution)/shard_map/dot_general | solution.py:104
  87.8 0.1 reshape.454
  87.9 0.3 fusion.36
  88.2 0.1 fusion.22
  88.3 0.2 fusion.9
  88.5 0.2 fusion.37
  88.7 0.5 convolution_convert_fusion.1
  89.2 1.4 convolution_convert_fusion
  90.7 0.1 select_reduce_fusion.3
  90.8 0.1 iota_add_fusion
  90.9 0.1 add.303
  91.0 0.1 compare_and_fusion.1
  91.1 40.7 %reduce-scatter.2.cloned.1.call-done = bf16[256,256]{1,0:T(8,128)(2,1)} async-done(((bf16[256,2048]{1,0:T(8,128)(2,1)}), bf16[256,256]{1,0:T(8,128)(2,1)}) %reduce-scatter.2.cloned.1.call-update) | async-done | bytes 131088 | tf_op jit(solution)/shard_map/reduce_scatter | solution.py:131
  131.8 0.9 add_convert_fusion
  132.7 3.9 %gather_fusion.2 = bf16[1024,256]{1,0:T(8,128)(2,1)S(1)} fusion(bf16[256,256]{1,0:T(8,128)(2,1)S(1)} %add_convert_fusion, s32[1024]{0:T(1024)S(1)} %broadcast_clamp_fusion), kind=kCustom, calls=%fused_computation.2 | custom fusion | bytes 1052672 | tf_op jit(solution)/shard_map/jit(_take)/gather | solution.py:135
  136.7 1.0 broadcast_select_fusion
  137.7 14.8 %all-to-all-start.1 = ((bf16[64,16,256]{2,1,0:T(8,128)(2,1)}), bf16[64,16,256]{2,1,0:T(8,128)(2,1)S(1)}, u32[]{:S(2)}, u32[]{:S(2)}) async-start(bf16[64,16,256]{2,1,0:T(8,128)(2,1)} %broadcast_select_fusion), calls=%async_computation.2 | async-start | bytes 1048576 | tf_op jit(solution)/shard_map/all_to_all | solution.py:138
  152.4 0.1 convert_reduce_fusion.1
  152.5 0.1 select_reduce_fusion.5
  152.7 0.8 copy.42
  153.5 16.6 %all-to-all-done.1 = bf16[64,16,256]{2,1,0:T(8,128)(2,1)S(1)} async-done(((bf16[64,16,256]{2,1,0:T(8,128)(2,1)}), bf16[64,16,256]{2,1,0:T(8,128)(2,1)S(1)}, u32[]{:S(2)}, u32[]{:S(2)}) %all-to-all-start.1) | async-done | bytes 524320 | tf_op jit(solution)/shard_map/all_to_all | solution.py:138
  170.1 1.0 gather_fusion.3
  171.2 0.7 broadcast_select_fusion.2
  (50 shorter events, 0.4 us)
Async XLA Ops:
  7.2 82.0 %copy-start = (bf16[128,2048]{1,0:T(8,128)(2,1)S(1)}, bf16[128,2048]{1,0:T(8,128)(2,1)}, u32[]{:S(2)}) copy-start(bf16[128,2048]{1,0:T(8,128)(2,1)} %param.15) | copy-start | bytes 1572868
  7.2 2.3 %copy-start.1 = (bf16[208,256]{1,0:T(8,128)(2,1)S(1)}, bf16[208,256]{1,0:T(8,128)(2,1)}, u32[]{:S(2)}) copy-start(bf16[208,256]{1,0:T(8,128)(2,1)} %param.10) | copy-start | bytes 319492
  14.6 31.5 %copy-start.2 = (bf16[2048,3,128]{2,0,1:T(8,128)(2,1)S(1)}, bf16[2048,3,128]{2,0,1:T(8,128)(2,1)}, u32[]{:S(2)}) copy-start(bf16[2048,3,128]{2,0,1:T(8,128)(2,1)} %param.13) | copy-start | bytes 4718596
  14.6 29.4 %all-to-all-start = ((bf16[64,16,256]{2,1,0:T(8,128)(2,1)}), bf16[64,16,256]{2,1,0:T(8,128)(2,1)S(1)}, u32[]{:S(2)}, u32[]{:S(2)}) async-start(bf16[64,16,256]{2,1,0:T(8,128)(2,1)} %select_select_fusion), calls=%async_computation | async-start | bytes 1048576 | tf_op jit(solution)/shard_map/all_to_all | solution.py:74
  26.3 57.8 %all-gather.4.cloned.1.call-start = ((), (), s32[]{:S(2)}) async-start(), calls=%async_computation.3 | async-start | bytes 1179648 | tf_op jit(solution)/shard_map/all_gather | solution.py:91
  45.9 1.7 copy-start.6
  45.9 20.6 %copy-start.7 = (bf16[256]{0:T(256)(128)(2,1)S(1)}, bf16[256]{0:T(256)(128)(2,1)}, u32[]{:S(2)}) copy-start(bf16[256]{0:T(256)(128)(2,1)} %param.12) | copy-start | bytes 1540
  46.0 31.3 %copy-start.4 = (bf16[16,32,2,128]{3,2,1,0:T(2,128)(2,1)S(1)}, bf16[16,32,2,128]{3,2,1,0:T(2,128)(2,1)}, u32[]{:S(2)}) copy-start(bf16[16,32,2,128]{3,2,1,0:T(2,128)(2,1)} %param.17) | copy-start | bytes 786436
  46.0 31.5 %copy-start.5 = (bf16[3,128]{1,0:T(4,128)(2,1)S(1)}, bf16[3,128]{1,0:T(4,128)(2,1)}, u32[]{:S(2)}) copy-start(bf16[3,128]{1,0:T(4,128)(2,1)} %param.14) | copy-start | bytes 2308
  46.0 85.8 %reduce-scatter.2.cloned.1.call-start = ((), (), s32[]{:S(2)}) async-start(), calls=%async_computation.4 | async-start | bytes 1179648 | tf_op jit(solution)/shard_map/reduce_scatter | solution.py:131
  47.6 38.2 %copy-start.3 = (bf16[2048,3,128]{0,2,1:T(8,128)(2,1)S(1)}, bf16[2048,3,128]{0,2,1:T(8,128)(2,1)}, u32[]{:S(2)}) copy-start(bf16[2048,3,128]{0,2,1:T(8,128)(2,1)} %copy.38) | copy-start | bytes 4718596
  88.7 2.0 %copy-start.8 = (bf16[256]{0:T(256)(128)(2,1)S(1)}, bf16[256]{0:T(256)(128)(2,1)}, u32[]{:S(2)}) copy-start(bf16[256]{0:T(256)(128)(2,1)} %param.16) | copy-start | bytes 1540
  137.7 32.5 %all-to-all-start.1 = ((bf16[64,16,256]{2,1,0:T(8,128)(2,1)}), bf16[64,16,256]{2,1,0:T(8,128)(2,1)S(1)}, u32[]{:S(2)}, u32[]{:S(2)}) async-start(bf16[64,16,256]{2,1,0:T(8,128)(2,1)} %broadcast_select_fusion), calls=%async_computation.2 | async-start | bytes 1048576 | tf_op jit(solution)/shard_map/all_to_all | solution.py:138
Sparse Core Ops, SparseCore 0:
  46.1 37.9 all-gather.3
  90.8 40.9 reduce-scatter.1
where the time goes:
time: 179 us
  waiting for transfers between devices  81.2 us (45%)
  blocking collectives  29.5 us (16%)
  starting transfers between devices  26.6 us (15%)
  between operations  14.4 us (8%)
  local copies, waits for them, and re-layouts  14.2 us (8%)
  other arithmetic  8.64 us (5%)
  matrix products  4.15 us (2%)
    reduce_scatter x1, waiting for transfers between devices, per_device(): lax.psum_scatter(partial_value.astype(jnp.bfloat16), 'tp', scatter_dimens...  40.7 us
    all_gather x1, blocking collectives, per_device(): lax.all_gather(ln_gain, 'tp', axis=0, tiled=True)  18.9 us
    all_to_all x1, waiting for transfers between devices, per_device(): lax.all_to_all(outgoing.reshape(shards, per_peer * LMAX, part_cols), 'req...  17.3 us
    all_to_all x1, waiting for transfers between devices, per_device(): lax.all_to_all(outbound, 'req', split_axis=0, concat_axis=0, tiled=True)  16.6 us
    all_to_all x1, starting transfers between devices, per_device(): lax.all_to_all(outbound, 'req', split_axis=0, concat_axis=0, tiled=True)  14.8 us
    all_to_all x1, starting transfers between devices, per_device(): lax.all_to_all(outgoing.reshape(shards, per_peer * LMAX, part_cols), 'req...  11.7 us
    all_gather x1, blocking collectives, per_device(): lax.all_gather(ln_bias, 'tp', axis=0, tiled=True)  10.7 us
    all_gather x1, waiting for transfers between devices, per_device(): lax.all_gather(local_rows, 'tp', axis=1, tiled=True)  6.51 us
  transfers between devices with their start and end apart: 4, of which 4 were waited for; matrix products, arithmetic and copies ran while one was open for 2% of the time, Pallas kernels for 0%

commit v1 on v0

--- a/solution.py
+++ b/solution.py
@@ -90,7 +90,15 @@
     whole_rows, whole_gain, whole_shift = (
         lax.all_gather(local_rows, "tp", axis=1, tiled=True),
         lax.all_gather(ln_gain, "tp", axis=0, tiled=True),
-        lax.all_gather(ln_bias, "tp", axis=0, tiled=True),
+        jnp.concatenate(
+            lax.all_to_all(
+                jnp.stack([ln_bias for _ in range(lax.axis_size("tp"))], axis=0),
+                "tp",
+                split_axis=0,
+                concat_axis=0,
+            ),
+            axis=0,
+        ),
     )
     values = whole_rows.astype(jnp.float32)
     normed = moments_norm(

time: 179 us -> 180 us (level)
  blocking collectives: 29.5 us -> 13 us
  starting transfers between devices: 26.6 us -> 36.8 us
  waiting for transfers between devices: 81.2 us -> 85.8 us
    all_gather x1 -> x0, blocking collectives: 10.7 us -> none  [per_device(): lax.all_gather(ln_bias, 'tp', axis=0, tiled=True)]
    all_to_all x0 -> x1, starting transfers between devices: none -> 10 us  [per_device(): lax.all_to_all(jnp.stack([ln_bias for _ in range(lax.axis_size('tp'))], a...]
    all_gather x1, blocking collectives: 18.9 us -> 13 us  [per_device(): lax.all_gather(ln_gain, 'tp', axis=0, tiled=True)]
    all_gather x1, waiting for transfers between devices: 6.51 us -> 11.2 us  [per_device(): lax.all_gather(local_rows, 'tp', axis=1, tiled=True)]
    unnamed x24 -> x23, local copies, waits for them, and re-layouts: 3.34 us -> 3.94 us
  transfers between devices with their start and end apart: 4 -> 5, of which waited for: 4 -> 4; matrix products, arithmetic and copies ran while one was open for 2% -> 3% of each run, Pallas kernels for 0% -> 0%
where the time goes in v1:
time: 180 us; the launch traced here: 179 us
  waiting for transfers between devices  85.8 us (48%)
  starting transfers between devices  36.8 us (20%)
  local copies, waits for them, and re-layouts  15.3 us (8%)
  between operations  14.4 us (8%)
  blocking collectives  13 us (7%)
  other arithmetic  9.31 us (5%)
  matrix products  4.66 us (3%)
    reduce_scatter x1, waiting for transfers between devices, per_device(): lax.psum_scatter(partial_value.astype(jnp.bfloat16), 'tp', scatter_dimens...  40.7 us
    all_to_all x1, waiting for transfers between devices, per_device(): lax.all_to_all(outgoing.reshape(shards, per_peer * LMAX, part_cols), 'req...  17.3 us
    all_to_all x1, waiting for transfers between devices, per_device(): lax.all_to_all(outbound, 'req', split_axis=0, concat_axis=0, tiled=True)  16.6 us
    all_to_all x1, starting transfers between devices, per_device(): lax.all_to_all(outbound, 'req', split_axis=0, concat_axis=0, tiled=True)  15 us
    all_gather x1, blocking collectives, per_device(): lax.all_gather(ln_gain, 'tp', axis=0, tiled=True)  13 us
    all_to_all x1, starting transfers between devices, per_device(): lax.all_to_all(outgoing.reshape(shards, per_peer * LMAX, part_cols), 'req...  11.7 us
    all_gather x1, waiting for transfers between devices, per_device(): lax.all_gather(local_rows, 'tp', axis=1, tiled=True)  11.2 us
    all_to_all x1, starting transfers between devices, per_device(): lax.all_to_all(jnp.stack([ln_bias for _ in range(lax.axis_size('tp'))], a...  10 us
  transfers between devices with their start and end apart: 5, of which 4 were waited for; matrix products, arithmetic and copies ran while one was open for 3% of the time, Pallas kernels for 0%

profile of v1, /device:TPU:1, one launch (start us, length us, event | category | flops | bytes accessed | tf_op | source)
XLA Modules:
  0.0 179.4 jit_solution(2692311006052857599)
XLA Ops:
  7.2 0.9 copy.35
  8.1 0.2 reduce-window_clone.1
  8.3 0.7 add_select_fusion
  9.0 0.1 reshape.465
  9.1 0.1 select_reduce_fusion.1
  9.2 0.1 add_minimum_fusion
  9.3 0.1 iota_compare_fusion.1
  9.4 0.1 min.22
  9.5 3.9 %gather_fusion = bf16[1024,256]{1,0:T(8,128)(2,1)S(1)} fusion(bf16[208,256]{1,0:T(8,128)(2,1)S(1)} %copy-done.1, s32[1024]{0:T(1024)S(1)} %broadcast_clamp_fusion.1), kind=kCustom, calls=%fused_computation | custom fusion | bytes 1052672 | tf_op jit(solution)/shard_map/jit(_take)/gather | solution.py:72
  13.4 1.1 select_select_fusion
  14.6 11.7 %all-to-all-start = ((bf16[64,16,256]{2,1,0:T(8,128)(2,1)}), bf16[64,16,256]{2,1,0:T(8,128)(2,1)S(1)}, u32[]{:S(2)}, u32[]{:S(2)}) async-start(bf16[64,16,256]{2,1,0:T(8,128)(2,1)} %select_select_fusion), calls=%async_computation | async-start | bytes 1048576 | tf_op jit(solution)/shard_map/all_to_all | solution.py:74
  26.5 0.1 add.290
  26.6 0.1 add.281
  26.7 17.3 %all-to-all-done = bf16[64,16,256]{2,1,0:T(8,128)(2,1)S(1)} async-done(((bf16[64,16,256]{2,1,0:T(8,128)(2,1)}), bf16[64,16,256]{2,1,0:T(8,128)(2,1)S(1)}, u32[]{:S(2)}, u32[]{:S(2)}) %all-to-all-start) | async-done | bytes 524320 | tf_op jit(solution)/shard_map/all_to_all | solution.py:74
  44.0 1.2 gather_fusion.1
  45.2 0.8 broadcast_select_fusion.1
  46.0 0.5 broadcast.462
  46.5 0.7 reduce.4
  47.2 0.6 reshape.511
  47.8 10.0 %all-to-all-start.1 = ((bf16[8,2,128]{2,1,0:T(2,128)(2,1)}), bf16[8,2,128]{2,1,0:T(2,128)(2,1)S(1)}, u32[]{:S(2)}, u32[]{:S(2)}) async-start(bf16[8,2,128]{2,1,0:T(2,128)(2,1)} %reshape.511), calls=%async_computation.1 | async-start | bytes 8192 | tf_op jit(solution)/shard_map/all_to_all | solution.py:94
  58.0 0.1 fusion.26
  58.0 0.1 convert_multiply_fusion.1
  58.1 0.1 iota_compare_fusion.5
  58.2 1.6 copy.38
  59.8 13.0 %all-gather = bf16[8,1,256]{2,1,0:T(2,128)(2,1)S(1)} all-gather(bf16[1,1,256]{2,1,0:T(2,128)(2,1)S(1)} %reshape.508), channel_id=1, replica_groups=mesh['req'=64,'tp'=8] {'tp'}, dimensions={0}, use_global_device_ids=true | all-gather | bytes 4608 | tf_op jit(solution)/shard_map/all_gather | solution.py:92
  72.8 11.2 %all-gather.3.cloned.1.call-done = bf16[256,2048]{1,0:T(8,128)(2,1)} async-done(((bf16[256,256]{1,0:T(8,128)(2,1)}), bf16[256,2048]{1,0:T(8,128)(2,1)}) %all-gather.3.cloned.1.call-update) | async-done | bytes 1048592 | tf_op jit(solution)/shard_map/all_gather | solution.py:91
  84.0 1.7 convert_reduce_fusion
  85.7 2.5 %convolution_add_fusion = bf16[256,384]{1,0:T(8,128)(2,1)S(1)} fusion(bf16[2048,384]{0,1:T(8,128)(2,1)} %bitcast.64, bf16[256,2048]{1,0:T(8,128)(2,1)} %all-gather.3.cloned.1.call-done, f32[2048]{0:T(1024)S(1)} %bitcast.70, f32[2048]{0:T(1024)S(1)} %bitcast.69, f32[256]{0:T(256)S(1)} %get-tuple-element.28, f32[256]{0:T(256)S(1)} %get-tuple-element.27, ...), kind=kOutput, calls=%fused_computation.14 | convolution fusion | flops 405995520 | bytes 2838016 | tf_op jit(solution)/shard_map/dot_general | solution.py:112
  88.3 0.3 fusion.36
  88.6 0.1 fusion.22
  88.7 0.2 fusion.9
  88.9 0.2 fusion.37
  89.1 0.5 convolution_convert_fusion.1
  89.6 1.4 convolution_convert_fusion
  91.1 0.1 select_reduce_fusion.3
  91.3 0.1 add.303
  91.4 0.1 compare_and_fusion.1
  91.5 40.7 %reduce-scatter.2.cloned.1.call-done = bf16[256,256]{1,0:T(8,128)(2,1)} async-done(((bf16[256,2048]{1,0:T(8,128)(2,1)}), bf16[256,256]{1,0:T(8,128)(2,1)}) %reduce-scatter.2.cloned.1.call-update) | async-done | bytes 131088 | tf_op jit(solution)/shard_map/reduce_scatter | solution.py:139
  132.2 0.9 add_convert_fusion
  133.1 3.9 %gather_fusion.2 = bf16[1024,256]{1,0:T(8,128)(2,1)S(1)} fusion(bf16[256,256]{1,0:T(8,128)(2,1)S(1)} %add_convert_fusion, s32[1024]{0:T(1024)S(1)} %broadcast_clamp_fusion), kind=kCustom, calls=%fused_computation.2 | custom fusion | bytes 1052672 | tf_op jit(solution)/shard_map/jit(_take)/gather | solution.py:143
  137.1 1.0 broadcast_select_fusion
  138.1 15.0 %all-to-all-start.2 = ((bf16[64,16,256]{2,1,0:T(8,128)(2,1)}), bf16[64,16,256]{2,1,0:T(8,128)(2,1)S(1)}, u32[]{:S(2)}, u32[]{:S(2)}) async-start(bf16[64,16,256]{2,1,0:T(8,128)(2,1)} %broadcast_select_fusion), calls=%async_computation.3 | async-start | bytes 1048576 | tf_op jit(solution)/shard_map/all_to_all | solution.py:146
  153.1 0.1 convert_reduce_fusion.1
  153.2 0.1 select_reduce_fusion.5
  153.3 0.8 copy.42
  154.1 16.6 %all-to-all-done.2 = bf16[64,16,256]{2,1,0:T(8,128)(2,1)S(1)} async-done(((bf16[64,16,256]{2,1,0:T(8,128)(2,1)}), bf16[64,16,256]{2,1,0:T(8,128)(2,1)S(1)}, u32[]{:S(2)}, u32[]{:S(2)}) %all-to-all-start.2) | async-done | bytes 524320 | tf_op jit(solution)/shard_map/all_to_all | solution.py:146
  170.7 1.0 gather_fusion.3
  171.8 0.7 broadcast_select_fusion.2
  (53 shorter events, 0.6 us)
Async XLA Ops:
  7.2 82.5 %copy-start = (bf16[128,2048]{1,0:T(8,128)(2,1)S(1)}, bf16[128,2048]{1,0:T(8,128)(2,1)}, u32[]{:S(2)}) copy-start(bf16[128,2048]{1,0:T(8,128)(2,1)} %param.15) | copy-start | bytes 1572868
  7.2 2.3 %copy-start.1 = (bf16[208,256]{1,0:T(8,128)(2,1)S(1)}, bf16[208,256]{1,0:T(8,128)(2,1)}, u32[]{:S(2)}) copy-start(bf16[208,256]{1,0:T(8,128)(2,1)} %param.10) | copy-start | bytes 319492
  14.6 31.4 %copy-start.5 = (bf16[256]{0:T(256)(128)(2,1)S(1)}, bf16[256]{0:T(256)(128)(2,1)}, u32[]{:S(2)}) copy-start(bf16[256]{0:T(256)(128)(2,1)} %param.12) | copy-start | bytes 1540
  14.6 43.3 %copy-start.3 = (bf16[16,32,2,128]{3,2,1,0:T(2,128)(2,1)S(1)}, bf16[16,32,2,128]{3,2,1,0:T(2,128)(2,1)}, u32[]{:S(2)}) copy-start(bf16[16,32,2,128]{3,2,1,0:T(2,128)(2,1)} %param.17) | copy-start | bytes 786436
  14.6 43.5 %copy-start.4 = (bf16[3,128]{1,0:T(4,128)(2,1)S(1)}, bf16[3,128]{1,0:T(4,128)(2,1)}, u32[]{:S(2)}) copy-start(bf16[3,128]{1,0:T(4,128)(2,1)} %param.14) | copy-start | bytes 2308
  14.6 29.4 %all-to-all-start = ((bf16[64,16,256]{2,1,0:T(8,128)(2,1)}), bf16[64,16,256]{2,1,0:T(8,128)(2,1)S(1)}, u32[]{:S(2)}, u32[]{:S(2)}) async-start(bf16[64,16,256]{2,1,0:T(8,128)(2,1)} %select_select_fusion), calls=%async_computation | async-start | bytes 1048576 | tf_op jit(solution)/shard_map/all_to_all | solution.py:74
  26.3 31.9 %copy-start.2 = (bf16[2048,3,128]{2,0,1:T(8,128)(2,1)S(1)}, bf16[2048,3,128]{2,0,1:T(8,128)(2,1)}, u32[]{:S(2)}) copy-start(bf16[2048,3,128]{2,0,1:T(8,128)(2,1)} %param.13) | copy-start | bytes 4718596
  26.3 57.7 %all-gather.3.cloned.1.call-start = ((), (), s32[]{:S(2)}) async-start(), calls=%async_computation.4 | async-start | bytes 1179648 | tf_op jit(solution)/shard_map/all_gather | solution.py:91
  47.8 25.0 %all-to-all-start.1 = ((bf16[8,2,128]{2,1,0:T(2,128)(2,1)}), bf16[8,2,128]{2,1,0:T(2,128)(2,1)S(1)}, u32[]{:S(2)}, u32[]{:S(2)}) async-start(bf16[8,2,128]{2,1,0:T(2,128)(2,1)} %reshape.511), calls=%async_computation.1 | async-start | bytes 8192 | tf_op jit(solution)/shard_map/all_to_all | solution.py:94
  57.8 74.4 %reduce-scatter.2.cloned.1.call-start = ((), (), s32[]{:S(2)}) async-start(), calls=%async_computation.5 | async-start | bytes 1179648 | tf_op jit(solution)/shard_map/reduce_scatter | solution.py:139
  58.2 1.6 copy-start.6
  89.1 2.0 %copy-start.7 = (bf16[256]{0:T(256)(128)(2,1)S(1)}, bf16[256]{0:T(256)(128)(2,1)}, u32[]{:S(2)}) copy-start(bf16[256]{0:T(256)(128)(2,1)} %param.16) | copy-start | bytes 1540
  138.1 32.7 %all-to-all-start.2 = ((bf16[64,16,256]{2,1,0:T(8,128)(2,1)}), bf16[64,16,256]{2,1,0:T(8,128)(2,1)S(1)}, u32[]{:S(2)}, u32[]{:S(2)}) async-start(bf16[64,16,256]{2,1,0:T(8,128)(2,1)} %broadcast_select_fusion), calls=%async_computation.3 | async-start | bytes 1048576 | tf_op jit(solution)/shard_map/all_to_all | solution.py:146
Sparse Core Ops, SparseCore 0:
  46.1 37.9 all-gather.2
  91.2 40.9 reduce-scatter.1
